TPU v7x, 128 devices: a whole 4x4x4 slice. The times are simulated.
128 devices in a mesh: ctx: 16 (over x, z), head: 8 (over y, core).
Axes of the slice: x: 4, y: 4, z: 4, core: 2. Of those that a mesh axis runs over, the one named last changes fastest.
Arguments:
- queries: bfloat16 [64, 8192], P('ctx', 'head'), may hold values from -16 to 16
- keys: bfloat16 [524288, 8, 128], P('ctx', 'head'), may hold values from -16 to 16
- values: bfloat16 [524288, 8, 128], P('ctx', 'head'), may hold values from -4 to 4
- offsets: int32 [16], P('ctx'), may hold values from 0 to 491520, as said below
- lengths: int32 [64], replicated, may hold values from 262144 to 524288
- residual: bfloat16 [64, 5120], P(None, 'ctx'), may hold values from -2 to 2
- wo: bfloat16 [8192, 5120], P('head', 'ctx'), may hold values from -0.0625 to 0.0625
- norm_gain: float32 [5120], P('ctx'), may hold values from 0.1 to 1.9
- w_gate: bfloat16 [5120, 25600], P('ctx', 'head'), may hold values from -0.078125 to 0.078125
- w_up: bfloat16 [5120, 25600], P('ctx', 'head'), may hold values from -0.078125 to 0.078125
- w_down: bfloat16 [25600, 5120], P('head', 'ctx'), may hold values from -0.0390625 to 0.0390625
Outputs:
- attended: bfloat16 [64, 8192], P('ctx', 'head')
- stream: bfloat16 [64, 5120], P(None, 'ctx')
- ffn_out: bfloat16 [64, 5120], P('head', 'ctx')
Inputs may be any that keep to these rules, and one draw needn't show every extreme that they name: offsets holds each of 0, 32768, ..., 491520 once.
All inputs are finite; a program needn't handle non-finite values.
Results may differ from a plain program's by a relative error of at most 0.02.
Values may be sent and summed in bfloat16 or wider, within the bound.
A program may use at most 128 MiB of HBM per device.

v0:
```python
import math

import jax
import jax.numpy as jnp
from jax import lax
from jax.sharding import PartitionSpec as P

D = 5120


masked_score = -1e30
epsilon = 1e-06


def activate(gate, upward, square_total):
    scale = lax.rsqrt(square_total / D + epsilon)[:, None]
    return (jax.nn.silu(scale * gate) * (scale * upward)).astype(jnp.bfloat16)


def local(queries, keys, values, offsets, lengths, residual, wo, norm_gain, w_gate, w_up, w_down):
    head_size = keys.shape[2]
    kv_local = keys.shape[1]
    rows_local = queries.shape[0]
    everyone = lax.all_gather(queries, "ctx", axis=0, tiled=True)
    batch = everyone.shape[0]
    groups = everyone.shape[1] // (kv_local * head_size)
    query_heads = everyone.reshape(batch, kv_local, groups, head_size)
    query_heads = query_heads.transpose(1, 0, 2, 3).reshape(kv_local, batch * groups, head_size)
    row_limit = jnp.repeat(lengths, groups)
    inverse_root = 1.0 / math.sqrt(head_size)
    span = keys.shape[0]
    block = min(2048, span)
    turns = span // block
    shard_begin = offsets[0]

    def visit(carry, block_index):
        row_high, row_total, row_acc = carry
        first_slot = block_index * block
        key_block = lax.dynamic_slice_in_dim(keys, first_slot, block, 0)
        value_block = lax.dynamic_slice_in_dim(values, first_slot, block, 0)
        scores = (
            jnp.einsum("hrd,khd->hrk", query_heads, key_block, preferred_element_type=jnp.float32)
            * inverse_root
        )
        position = shard_begin + first_slot + jnp.arange(block, dtype=jnp.int32)
        scores = jnp.where(position[None, None, :] < row_limit[None, :, None], scores, masked_score)
        new_high = jnp.maximum(row_high, jnp.max(scores, axis=2))
        weights = jnp.exp(scores - new_high[:, :, None])
        rescale = jnp.exp(row_high - new_high)
        row_total = row_total * rescale + jnp.sum(weights, axis=2)
        update = jnp.einsum(
            "hrk,khd->hrd",
            weights.astype(jnp.bfloat16),
            value_block,
            preferred_element_type=jnp.float32,
        )
        row_acc = row_acc * rescale[:, :, None] + update
        return ((new_high, row_total, row_acc), None)

    start_high = jnp.full((kv_local, batch * groups), masked_score, jnp.float32)
    start_total = jnp.zeros((kv_local, batch * groups), jnp.float32)
    start_acc = jnp.zeros((kv_local, batch * groups, head_size), jnp.float32)
    (row_high, row_total, row_acc), _ = lax.scan(
        visit, (start_high, start_total, start_acc), jnp.arange(turns, dtype=jnp.int32)
    )
    heads_local = kv_local * groups
    row_high = (
        row_high.reshape(kv_local, batch, groups).transpose(1, 0, 2).reshape(batch, heads_local)
    )
    row_total = (
        row_total.reshape(kv_local, batch, groups).transpose(1, 0, 2).reshape(batch, heads_local)
    )
    row_acc = (
        row_acc.reshape(kv_local, batch, groups, head_size)
        .transpose(1, 0, 2, 3)
        .reshape(batch, heads_local, head_size)
    )
    top_score = lax.pmax(row_high, "ctx")
    rescale = jnp.exp(row_high - top_score)
    summed_acc, summed_total = lax.psum((row_acc * rescale[:, :, None], row_total * rescale), "ctx")
    whole_rows = (
        (summed_acc / summed_total[:, :, None])
        .reshape(batch, heads_local * head_size)
        .astype(jnp.bfloat16)
    )
    attended = lax.dynamic_slice_in_dim(
        whole_rows, lax.axis_index("ctx") * rows_local, rows_local, 0
    )
    projected = jnp.dot(whole_rows, wo, preferred_element_type=jnp.float32)
    mixed = lax.psum(projected, "head")
    combined = residual.astype(jnp.float32) + mixed
    stream = combined.astype(jnp.bfloat16)
    squares = jnp.sum(combined * combined, axis=1)
    normed = (combined * norm_gain).astype(jnp.bfloat16)
    gate_part = jnp.dot(normed, w_gate, preferred_element_type=jnp.float32)
    up_part = jnp.dot(normed, w_up, preferred_element_type=jnp.float32)
    square_total = lax.psum(squares, "ctx")
    gate, upward = lax.psum((gate_part, up_part), "ctx")
    hidden = activate(gate, upward, square_total)
    ffn_out = lax.psum_scatter(
        jnp.dot(hidden, w_down, preferred_element_type=jnp.float32),
        "head",
        scatter_dimension=0,
        tiled=True,
    ).astype(jnp.bfloat16)
    return (attended, stream, ffn_out)


def solution(mesh):
    return jax.shard_map(
        local,
        mesh=mesh,
        in_specs=(
            P("ctx", "head"),
            P("ctx", "head", None),
            P("ctx", "head", None),
            P("ctx"),
            P(),
            P(None, "ctx"),
            P("head", "ctx"),
            P("ctx"),
            P("ctx", "head"),
            P("ctx", "head"),
            P("head", "ctx"),
        ),
        out_specs=(P("ctx", "head"), P(None, "ctx"), P("head", "ctx")),
        check_vma=False,
    )
```

profile of v0, /device:TPU:1, one launch (start us, length us, event | category | flops | bytes accessed | tf_op | source)
XLA Modules:
  0.0 565.0 jit_solution(13764307791366499281)
XLA Ops:
  7.3 20.8 %all-gather = bf16[16,4,1024]{2,1,0:T(4,128)(2,1)S(1)} all-gather(bf16[1,4,1024]{2,1,0:T(4,128)(2,1)} %bitcast.66), channel_id=1, replica_groups=mesh['ctx'=16,'head'=8] {'ctx'}, dimensions={0}, use_global_device_ids=true | all-gather | bytes 139264 | tf_op jit(solution)/shard_map/all_gather | solution.py:24
  28.2 189.1 %while.15 = (s32[]{:T(128)}, f32[1,512]{1,0:T(1,128)S(1)}, f32[1,512]{1,0:T(1,128)S(1)}, f32[1,512,128]{2,1,0:T(8,128)S(1)}, s32[16]{0:T(128)S(1)}, /*index=5*/s...) while((s32[]{:T(128)}, f32[1,512]{1,0:T(1,128)S(1)}, ...), condition=%wide.region_3.4_spmd.clone, body=%wide.region_0.3_spmd.clone.sunk | while | flops 545460736 | bytes 31121916 | solution.py:63
  30.9 3.7 fusion.46
  42.7 3.7 fusion.46
  54.5 3.7 fusion.46
  66.3 3.7 fusion.46
  78.2 3.7 fusion.46
  90.0 3.7 fusion.46
  101.8 3.7 fusion.46
  113.6 3.7 fusion.46
  125.4 3.7 fusion.46
  137.3 3.7 fusion.46
  149.1 3.7 fusion.46
  160.9 3.7 fusion.46
  172.7 3.7 fusion.46
  184.5 3.7 fusion.46
  196.3 3.7 fusion.46
  218.5 57.9 %pmax.7 = f32[64,8]{1,0:T(8,128)S(1)} all-reduce(f32[64,8]{1,0:T(8,128)S(1)} %reshape_transpose_reshape.14), channel_id=1, replica_groups=mesh['ctx'=16,'head'=8] {'ctx'}, use_global_device_ids=true, to_apply=%region_4.5 | all-reduce | flops 512 | bytes 4096 | tf_op jit(solution)/shard_map/pmax | solution.py:78
  278.1 55.8 %psum.43 = f32[64,8]{1,0:T(8,128)S(1)} all-reduce(f32[64,8]{1,0:T(8,128)S(1)} %get-tuple-element.120), channel_id=1, replica_groups=mesh['ctx'=16,'head'=8] {'ctx'}, use_global_device_ids=true, to_apply=%region_6.7 | all-reduce | flops 512 | bytes 4096 | tf_op jit(solution)/shard_map/psum | solution.py:80
  333.9 43.2 %all-reduce.6.cloned.1.call-done = f32[64,8,128]{2,1,0:T(8,128)} async-done(((f32[64,8,128]{2,1,0:T(8,128)}), f32[64,8,128]{2,1,0:T(8,128)}) %all-reduce.6.cloned.1.call-update) | async-done | bytes 262160 | tf_op jit(solution)/shard_map/psum | solution.py:80
  379.3 57.6 %all-reduce.8.cloned.1.call-done = f32[64,320]{1,0:T(8,128)} async-done(((f32[64,320]{1,0:T(8,128)}), f32[64,320]{1,0:T(8,128)}) %all-reduce.8.cloned.1.call-update) | async-done | bytes 81936 | tf_op jit(solution)/shard_map/psum | solution.py:90
  445.0 33.4 %psum.45 = f32[64]{0:T(128)S(1)} all-reduce(f32[64]{0:T(128)S(1)} %get-tuple-element.124), channel_id=1, replica_groups=mesh['ctx'=16,'head'=8] {'ctx'}, use_global_device_ids=true, to_apply=%region_9.10 | all-reduce | flops 64 | bytes 512 | tf_op jit(solution)/shard_map/psum | solution.py:97
  478.4 53.1 %all-reduce.10.cloned.1.call-done = (f32[64,3200]{1,0:T(8,128)}, f32[64,3200]{1,0:T(8,128)}) async-done(((f32[64,3200]{1,0:T(8,128)}, f32[64,3200]{1,0:T(8,128)}), (f32[64,3200]{1,0:T(8,128)}, f32[64,3200]{1,0:T(8,128)})) %all-reduce.10.cloned.1.call-update) | async-done | bytes 1638416 | tf_op jit(solution)/shard_map/psum | solution.py:98
  534.3 23.6 %all-reduce = bf16[64,320]{1,0:T(8,128)(2,1)S(1)} all-reduce(f32[64,320]{1,0:T(8,128)S(1)} %fusion.23), channel_id=2, replica_groups=mesh['ctx'=16,'head'=8] {'head'}, use_global_device_ids=true, to_apply=%region_12.13.clone | all-reduce | flops 20480 | bytes 122880
  (216 shorter events, 128.0 us)
Async XLA Ops:
  7.2 431.4 %copy-start = (bf16[320,3200]{1,0:T(8,128)(2,1)S(1)}, bf16[320,3200]{1,0:T(8,128)(2,1)}, u32[]{:S(2)}) copy-start(bf16[320,3200]{1,0:T(8,128)(2,1)} %param.21) | copy-start | bytes 6144004
  7.2 370.0 %all-reduce.6.cloned.1.call-start = ((), (), s32[]{:S(2)}) async-start(), calls=%async_computation | async-start | bytes 524288 | tf_op jit(solution)/shard_map/psum | solution.py:80
  28.1 350.1 %copy-start.2 = (bf16[1024,320]{0,1:T(8,128)(2,1)S(1)}, bf16[1024,320]{0,1:T(8,128)(2,1)}, u32[]{:S(2)}) copy-start(bf16[1024,320]{0,1:T(8,128)(2,1)} %param.19) | copy-start | bytes 1966084
  28.1 408.8 %copy-start.3 = (bf16[64,320]{1,0:T(8,128)(2,1)S(1)}, bf16[64,320]{1,0:T(8,128)(2,1)}, u32[]{:S(2)}) copy-start(bf16[64,320]{1,0:T(8,128)(2,1)} %param.18) | copy-start | bytes 122884
  28.1 408.8 %copy-start.4 = (f32[320]{0:T(512)S(1)}, f32[320]{0:T(512)}, u32[]{:S(2)}) copy-start(f32[320]{0:T(512)} %param.20) | copy-start | bytes 3844
  34.6 3.4 copy-start.1
  46.4 3.4 copy-start.1
  58.2 3.4 copy-start.1
  70.0 3.4 copy-start.1
  81.9 3.4 copy-start.1
  93.7 3.4 copy-start.1
  105.5 3.4 copy-start.1
  117.3 3.4 copy-start.1
  129.1 3.4 copy-start.1
  140.9 3.4 copy-start.1
  152.8 3.4 copy-start.1
  164.6 3.4 copy-start.1
  176.4 3.4 copy-start.1
  188.2 3.4 copy-start.1
  200.0 3.4 copy-start.1
  211.8 3.4 copy-start.1
  278.1 158.9 %all-reduce.8.cloned.1.call-start = ((), (), s32[]{:S(2)}) async-start(), calls=%async_computation.1 | async-start | bytes 196608 | tf_op jit(solution)/shard_map/psum | solution.py:90
  378.3 64.8 %copy-start.5 = (u32[128]{0:T(128)S(1)}, u32[128]{0:T(128)}, u32[]{:S(2)}) copy-start(u32[128]{0:T(128)} %constant.51) | copy-start | bytes 1540
  379.3 152.2 %all-reduce.10.cloned.1.call-start = ((), (), s32[]{:S(2)}) async-start(), calls=%async_computation.2 | async-start | bytes 3276800 | tf_op jit(solution)/shard_map/psum | solution.py:98
Sparse Core Ops, SparseCore 0:
  278.2 98.9 all-reduce.5
  379.5 57.4 all-reduce.7
  443.2 88.2 all-reduce.9
where the time goes:
time: 570 us; the launch traced here: 565 us
  blocking collectives  192 us (34%)
  waiting for transfers between devices  154 us (27%)
  matrix products  98 us (17%)
  other arithmetic  52.9 us (9%)
  local copies, waits for them, and re-layouts  32.3 us (6%)
  loops' own time  21.6 us (4%)
  between operations  14.6 us (3%)
    dot_general x16, matrix products, visit(): jnp.einsum('hrd,khd->hrk', query_heads, key_block, preferred_element_type...  59.1 us
    pmax x1, blocking collectives, local(): top_score = lax.pmax(row_high, 'ctx')  57.9 us
    psum x1, waiting for transfers between devices, local(): mixed = lax.psum(projected, 'head')  57.6 us
    psum x1, blocking collectives, local(): lax.psum((row_acc * rescale[:, :, None], row_total * rescale), 'ctx')  55.8 us
    psum x1, waiting for transfers between devices, local(): gate, upward = lax.psum((gate_part, up_part), 'ctx')  53.1 us
    reduce_sum x16, other arithmetic, visit(): row_total = row_total * rescale + jnp.sum(weights, axis=2)  47.5 us
    psum x1, waiting for transfers between devices, local(): lax.psum((row_acc * rescale[:, :, None], row_total * rescale), 'ctx')  43.2 us
    psum x1, blocking collectives, local(): square_total = lax.psum(squares, 'ctx')  33.4 us
  transfers between devices with their start and end apart: 3, of which 3 were waited for; matrix products, arithmetic and copies ran while one was open for 0% of the time, Pallas kernels for 0%

commit v1 on v0

v1 whole, which is shorter than its diff:
```python
import functools
import math

import jax
import jax.numpy as jnp
from jax import lax
from jax.experimental import pallas as pl
from jax.experimental.pallas import tpu as pltpu
from jax.sharding import PartitionSpec as P

MESH = pl.DeviceIdType.MESH
F32 = jnp.float32
BF16 = jnp.bfloat16
EPSILON = 1e-06
HIDDEN_SCORE = -1e30
GROUPS = 8
HEAD = 128
LANES = 128


def dot(a, b):
    return jnp.dot(a, b, preferred_element_type=F32)


def dot_across(a, b):
    return lax.dot_general(a, b, (((1,), (1,)), ((), ())), preferred_element_type=F32)


def kernel(
    sizes,
    queries,
    lengths,
    offsets,
    residual,
    gain,
    keys,
    values,
    wo,
    w_gate,
    w_up,
    w_down,
    attended,
    stream,
    ffn_out,
    key_buf,
    value_buf,
    wo_buf,
    pair_buf,
    down_buf,
    visible,
    query_row,
    query_send,
    query_all,
    query_wide,
    score_buf,
    high,
    total,
    acc,
    part_send,
    part_recv,
    rows_f32,
    rows_send,
    rows_all,
    wide_f32,
    proj_all,
    square_tile,
    lhs,
    gate_send,
    gate_recv,
    hidden_send,
    hidden_all,
    down_send,
    down_recv,
    load_sem,
    weight_sem,
    ctx_send,
    ctx_recv,
    head_send,
    head_recv,
):
    ctxs, heads, span, block, width, model = sizes
    batch = 4 * ctxs
    rows = batch * GROUPS
    turns = span // block
    hidden_width = w_gate.shape[1]
    first = pair_buf.shape[1]
    second = hidden_width - first
    base = 1.0 / math.sqrt(HEAD) * math.log2(math.e)
    ctx = lax.axis_index("ctx")
    head = lax.axis_index("head")

    def key_copy(c):
        part = pl.ds(pl.multiple_of(c * block, block), block)
        return pltpu.make_async_copy(keys.at[part], key_buf.at[part], load_sem.at[0, c])

    def value_copy(c):
        part = pl.ds(pl.multiple_of(c * block, block), block)
        return pltpu.make_async_copy(values.at[part], value_buf.at[part], load_sem.at[1, c])

    weight_copies = [
        pltpu.make_async_copy(wo, wo_buf, weight_sem.at[0]),
        pltpu.make_async_copy(
            w_gate.at[:, 0:first], pair_buf.at[0:width, :], weight_sem.at[1]
        ),
        pltpu.make_async_copy(
            w_up.at[:, 0:first], pair_buf.at[width : 2 * width, :], weight_sem.at[2]
        ),
        pltpu.make_async_copy(
            w_gate.at[:, first:hidden_width],
            pair_buf.at[2 * width : 3 * width, 0:second],
            weight_sem.at[3],
        ),
        pltpu.make_async_copy(
            w_up.at[:, first:hidden_width],
            pair_buf.at[3 * width : 4 * width, 0:second],
            weight_sem.at[4],
        ),
        pltpu.make_async_copy(w_down, down_buf, weight_sem.at[5]),
    ]

    barrier = pltpu.get_barrier_semaphore()

    def greet_ctx(p, _):
        pl.semaphore_signal(
            barrier, inc=1, device_id={"ctx": lax.rem(ctx + p, ctxs)}, device_id_type=MESH
        )
        return 0

    def greet_head(p, _):
        pl.semaphore_signal(
            barrier, inc=1, device_id={"head": lax.rem(head + p, heads)}, device_id_type=MESH
        )
        return 0

    lax.fori_loop(1, ctxs, greet_ctx, 0)
    lax.fori_loop(1, heads, greet_head, 0)

    def fetch(c, _):
        key_copy(c).start()
        value_copy(c).start()
        return 0

    lax.fori_loop(0, turns, fetch, 0)
    for copy in weight_copies:
        copy.start()

    def over_ctx(phase, source, slots):
        def one(other, mine):
            return pltpu.make_async_remote_copy(
                src_ref=source(other),
                dst_ref=slots.at[mine],
                send_sem=ctx_send.at[phase, other],
                recv_sem=ctx_recv.at[phase, mine],
                device_id={"ctx": other},
                device_id_type=MESH,
            )

        def start(p, _):
            one(lax.rem(ctx + p, ctxs), ctx).start()
            return 0

        def arrive(p, _):
            other = lax.rem(ctx + ctxs - p, ctxs)
            one(other, other).wait_recv()
            return 0

        def sent(p, _):
            one(lax.rem(ctx + p, ctxs), ctx).wait_send()
            return 0

        return (
            lambda: lax.fori_loop(1, ctxs, start, 0),
            lambda: lax.fori_loop(1, ctxs, arrive, 0),
            lambda: lax.fori_loop(1, ctxs, sent, 0),
        )

    def over_head(phase, source, slots):
        def one(other, mine):
            return pltpu.make_async_remote_copy(
                src_ref=source(other),
                dst_ref=slots.at[mine],
                send_sem=head_send.at[phase, other],
                recv_sem=head_recv.at[phase, mine],
                device_id={"head": other},
                device_id_type=MESH,
            )

        def start(p, _):
            one(lax.rem(head + p, heads), head).start()
            return 0

        def arrive(p, _):
            other = lax.rem(head + heads - p, heads)
            one(other, other).wait_recv()
            return 0

        def sent(p, _):
            one(lax.rem(head + p, heads), head).wait_send()
            return 0

        return (
            lambda: lax.fori_loop(1, heads, start, 0),
            lambda: lax.fori_loop(1, heads, arrive, 0),
            lambda: lax.fori_loop(1, heads, sent, 0),
        )

    own = queries[...].astype(F32)
    for g in range(GROUPS):
        query_row[pl.ds(g, 4, stride=GROUPS), :] = own[:, g * HEAD : (g + 1) * HEAD]
    query_send[...] = query_row[...].astype(BF16)
    query_all[ctx] = query_send[...]

    pl.semaphore_wait(barrier, ctxs - 1 + heads - 1)
    q_start, q_arrive, q_sent = over_ctx(0, lambda other: query_send, query_all)
    q_start()

    visible[...] = jnp.full(visible.shape, 2**30, jnp.int32)
    visible[0:1, 0:batch] = lengths[...] - offsets[0]
    high[...] = jnp.full(high.shape, -3e38, F32)
    total[...] = jnp.zeros(total.shape, F32)
    acc[...] = jnp.zeros(acc.shape, F32)
    row_of = lax.broadcasted_iota(jnp.int32, (rows, LANES), 0) // GROUPS
    column = lax.broadcasted_iota(jnp.int32, (rows, LANES), 1)
    query_wide[:, HEAD : HEAD + LANES] = jnp.where(row_of == column, HIDDEN_SCORE, 0.0).astype(BF16)
    q_arrive()
    query_wide[:, 0:HEAD] = query_all[...].reshape(rows, HEAD)

    def scores(c):
        part = pl.ds(pl.multiple_of(c * block, block), block)
        slot = lax.broadcasted_iota(jnp.int32, (block, LANES), 0)
        beyond = jnp.where(slot >= visible[0:1, :] - c * block, 1.0, 0.0).astype(BF16)
        return dot_across(
            jnp.concatenate([key_buf[part, :], beyond], axis=1), query_wide[...]
        )

    def absorb(c, slot):
        part = pl.ds(pl.multiple_of(c * block, block), block)
        s = score_buf[slot]
        old = high[0:1, :]
        new = jnp.maximum(old, jnp.max(s, axis=0, keepdims=True))
        weights = jnp.exp2((s - new) * base).astype(BF16)
        rescale = jnp.exp2((old - new) * base)
        high[...] = jnp.broadcast_to(new, high.shape)
        upright = jnp.concatenate(
            [value_buf[part, :].T, jnp.ones((16, block), BF16)], axis=0
        )
        update = dot(upright, weights)
        acc[...] = acc[...] * rescale + update[0:HEAD]
        total[...] = total[...] * rescale + update[HEAD : HEAD + 8]

    key_copy(0).wait()
    score_buf[0] = scores(0)

    def visit(i, _):
        c = 2 * i
        key_copy(c + 1).wait()
        value_copy(c).wait()
        key_copy(c + 2).wait()
        value_copy(c + 1).wait()
        score_buf[1] = scores(c + 1)
        absorb(c, 0)
        score_buf[0] = scores(c + 2)
        absorb(c + 1, 1)
        return 0

    lax.fori_loop(0, turns // 2 - 1, visit, 0)
    key_copy(turns - 1).wait()
    value_copy(turns - 2).wait()
    value_copy(turns - 1).wait()
    score_buf[1] = scores(turns - 1)
    absorb(turns - 2, 0)
    absorb(turns - 1, 1)

    high_row = high[0:1, :]
    total_row = total[0:1, :]
    part_send[:, 0:32, :] = (
        (acc[...] / total_row).T.astype(BF16).reshape(ctxs, 32, HEAD)
    )

    def piece(v):
        return v.astype(BF16).astype(F32)

    h1 = piece(high_row)
    h2 = piece(high_row - h1)
    h3 = piece(high_row - h1 - h2)
    t1 = piece(total_row)
    t2 = piece(total_row - t1)
    index = lax.broadcasted_iota(jnp.int32, (16, rows), 0)
    stats = jnp.zeros((16, rows), F32)
    for k, v in enumerate((h1, h2, h3, t1, t2)):
        stats = jnp.where(index == k, v, stats)
    stats = stats.astype(BF16)
    for i in range(ctxs):
        at = i // 4 * LANES
        part_send[i, 32:48, :] = stats[:, at : at + LANES]
    part_recv[ctx] = part_send[ctx]
    p_start, p_arrive, p_sent = over_ctx(1, lambda other: part_send.at[other], part_recv)
    p_start()
    q_sent()
    p_arrive()

    tops = []
    sums = []
    for i in range(ctxs):
        tile = part_recv[i, 32:48, :].astype(F32)
        tops.append(tile[0:1] + tile[1:2] + tile[2:3])
        sums.append(tile[3:4] + tile[4:5])
    tops = jnp.concatenate(tops, axis=0)
    sums = jnp.concatenate(sums, axis=0)
    shares = sums * jnp.exp2((tops - jnp.max(tops, axis=0, keepdims=True)) * base)
    shares = shares / jnp.sum(shares, axis=0, keepdims=True)
    square_tile[...] = jnp.zeros(square_tile.shape, F32)
    square_tile[0:ctxs, :] = shares
    square_tile[...] = square_tile[...].T
    mine = square_tile[pl.ds(pl.multiple_of(lax.rem(ctx, 4) * 32, 32), 32), :]
    merged = jnp.zeros((32, HEAD), F32)
    for i in range(ctxs):
        merged = merged + part_recv[i, 0:32, :].astype(F32) * mine[:, i : i + 1]
    rows_send[...] = merged.astype(BF16)
    rows_all[ctx] = rows_send[...]
    r_start, r_arrive, r_sent = over_ctx(2, lambda other: rows_send, rows_all)
    r_start()
    rows_f32[...] = rows_send[...].astype(F32)
    for g in range(GROUPS):
        attended[:, g * HEAD : (g + 1) * HEAD] = rows_f32[pl.ds(g, 4, stride=GROUPS), :].astype(
            BF16
        )
    p_sent()
    weight_copies[0].wait()
    r_arrive()

    wide_f32[...] = rows_all[...].astype(F32).reshape(rows, HEAD)
    projected = jnp.zeros((batch, width), F32)
    for g in range(GROUPS):
        lines = wide_f32[pl.ds(g, batch, stride=GROUPS), :].astype(BF16)
        projected = projected + dot_across(lines, wo_buf[:, g * HEAD : (g + 1) * HEAD])
    proj_all[head] = projected.astype(BF16)
    d_start, d_arrive, d_sent = over_head(0, lambda other: proj_all.at[head], proj_all)
    d_start()
    r_sent()
    d_arrive()

    combined = residual[...].astype(F32)
    mixed = proj_all[0].astype(F32)
    for i in range(1, heads):
        mixed = mixed + proj_all[i].astype(F32)
    combined = combined + mixed
    stream[...] = combined.astype(BF16)
    squares = jnp.sum(combined * combined, axis=1, keepdims=True)
    normed = (combined * gain[...]).astype(BF16)

    tall = 16 * ctxs
    spread = jnp.where(
        lax.broadcasted_iota(jnp.int32, (tall, batch), 0) // 16 * 4
        + lax.broadcasted_iota(jnp.int32, (tall, batch), 0) % 4
        == lax.broadcasted_iota(jnp.int32, (tall, batch), 1),
        1.0,
        0.0,
    ).astype(BF16)
    copies = dot(spread, normed)
    which = lax.broadcasted_iota(jnp.int32, (tall, width), 0) % 16 // 4
    for k in range(4):
        lhs[:, k * width : (k + 1) * width] = jnp.where(which == k, copies, 0.0).astype(BF16)
    s1 = squares.astype(BF16).astype(F32)
    s2 = squares - s1
    lane = lax.broadcasted_iota(jnp.int32, (batch, LANES), 1)
    marks = jnp.where(lane == 0, s1, jnp.where(lane == 1, s2, 0.0)).astype(BF16)
    gate_send[:, :, first : first + LANES] = (
        dot(spread, marks).astype(BF16).reshape(ctxs, 16, LANES)
    )
    for copy in weight_copies[1:5]:
        copy.wait()
    full = lhs[...]
    for at in range(0, second, 256):
        wide = min(256, second - at)
        gate_send[:, :, at : at + wide] = (
            dot(full, pair_buf[:, at : at + wide]).astype(BF16).reshape(ctxs, 16, wide)
        )
    gate_send[:, :, second:first] = (
        dot(full[:, 0 : 2 * width], pair_buf[0 : 2 * width, second:first])
        .astype(BF16)
        .reshape(ctxs, 16, first - second)
    )
    gate_recv[ctx] = gate_send[ctx]
    g_start, g_arrive, g_sent = over_ctx(3, lambda other: gate_send.at[other], gate_recv)
    g_start()
    d_sent()
    g_arrive()

    summed = gate_recv[0].astype(F32)
    for i in range(1, ctxs):
        summed = summed + gate_recv[i].astype(F32)
    square_total = jnp.sum(summed[:, first : first + LANES], axis=1, keepdims=True)
    scaled = summed[:, 0:first] * lax.rsqrt(square_total / model + EPSILON)

    def gated(v):
        return v / (1.0 + jnp.exp(-v)) * pltpu.roll(v, 4, 0)

    upper = gated(scaled[0:8])
    lower = gated(scaled[8:16])
    index = lax.broadcasted_iota(jnp.int32, (8, first), 0)
    hidden_send[...] = jnp.where(index < 4, upper, pltpu.roll(lower, 4, 0)).astype(BF16)
    hidden_all[ctx] = hidden_send[...]
    h_start, h_arrive, h_sent = over_ctx(4, lambda other: hidden_send, hidden_all)
    h_start()
    g_sent()
    weight_copies[5].wait()
    h_arrive()

    hidden = hidden_all[...].astype(F32).reshape(8 * ctxs, first).astype(BF16)
    one = dot_across(hidden, down_buf[:, 0:first])
    two = dot_across(hidden[:, 0:second], down_buf[:, first:hidden_width])
    both = one + pltpu.roll(two, 8 * ctxs - 4, 0)
    index = lax.broadcasted_iota(jnp.int32, (8, width), 0)
    for i in range(heads):
        down_send[i] = jnp.where(
            index < 4,
            both[16 * i : 16 * i + 8],
            pltpu.roll(both[16 * i + 8 : 16 * i + 16], 4, 0),
        )
    down_recv[head] = down_send[head]
    f_start, f_arrive, f_sent = over_head(1, lambda other: down_send.at[other], down_recv)
    f_start()
    h_sent()
    f_arrive()
    result = down_recv[0]
    for i in range(1, heads):
        result = result + down_recv[i]
    ffn_out[...] = result.astype(BF16)
    f_sent()


def local(
    ctxs,
    heads,
    block,
    queries,
    keys,
    values,
    offsets,
    lengths,
    residual,
    wo,
    norm_gain,
    w_gate,
    w_up,
    w_down,
):
    span = keys.shape[0]
    batch, width = residual.shape
    rows = batch * GROUPS
    hidden_width = w_gate.shape[1]
    first = (hidden_width // LANES + 1) // 2 * LANES
    sizes = (ctxs, heads, span, block, width, width * ctxs)
    vmem = pl.BlockSpec(memory_space=pltpu.VMEM)
    smem = pl.BlockSpec(memory_space=pltpu.SMEM)
    hbm = pl.BlockSpec(memory_space=pl.ANY)
    return pl.pallas_call(
        functools.partial(kernel, sizes),
        out_shape=(
            jax.ShapeDtypeStruct(queries.shape, BF16),
            jax.ShapeDtypeStruct((batch, width), BF16),
            jax.ShapeDtypeStruct((batch // heads, width), BF16),
        ),
        in_specs=[vmem, vmem, smem, vmem, vmem] + [hbm] * 6,
        out_specs=(vmem, vmem, vmem),
        scratch_shapes=[
            pltpu.VMEM((span, HEAD), BF16),
            pltpu.VMEM((span, HEAD), BF16),
            pltpu.VMEM((width, rows * HEAD // batch), BF16),
            pltpu.VMEM((4 * width, first), BF16),
            pltpu.VMEM((width, hidden_width), BF16),
            pltpu.VMEM((8, LANES), jnp.int32),
            pltpu.VMEM((32, HEAD), F32),
            pltpu.VMEM((32, HEAD), BF16),
            pltpu.VMEM((ctxs, 32, HEAD), BF16),
            pltpu.VMEM((rows, HEAD + LANES), BF16),
            pltpu.VMEM((2, block, rows), F32),
            pltpu.VMEM((8, rows), F32),
            pltpu.VMEM((8, rows), F32),
            pltpu.VMEM((HEAD, rows), F32),
            pltpu.VMEM((ctxs, 48, HEAD), BF16),
            pltpu.VMEM((ctxs, 48, HEAD), BF16),
            pltpu.VMEM((32, HEAD), F32),
            pltpu.VMEM((32, HEAD), BF16),
            pltpu.VMEM((ctxs, 32, HEAD), BF16),
            pltpu.VMEM((rows, HEAD), F32),
            pltpu.VMEM((heads, batch, width), BF16),
            pltpu.VMEM((LANES, LANES), F32),
            pltpu.VMEM((16 * ctxs, 4 * width), BF16),
            pltpu.VMEM((ctxs, 16, first + LANES), BF16),
            pltpu.VMEM((ctxs, 16, first + LANES), BF16),
            pltpu.VMEM((8, first), BF16),
            pltpu.VMEM((ctxs, 8, first), BF16),
            pltpu.VMEM((heads, 8, width), F32),
            pltpu.VMEM((heads, 8, width), F32),
            pltpu.SemaphoreType.DMA((2, span // block)),
            pltpu.SemaphoreType.DMA((6,)),
            pltpu.SemaphoreType.DMA((5, ctxs)),
            pltpu.SemaphoreType.DMA((5, ctxs)),
            pltpu.SemaphoreType.DMA((2, heads)),
            pltpu.SemaphoreType.DMA((2, heads)),
        ],
        compiler_params=pltpu.CompilerParams(
            collective_id=0, has_side_effects=True, vmem_limit_bytes=60 * 1024 * 1024
        ),
        name="layer",
    )(
        queries,
        lengths.reshape(1, batch),
        offsets,
        residual,
        norm_gain.reshape(1, width),
        keys.reshape(span, HEAD),
        values.reshape(span, HEAD),
        wo.T,
        w_gate,
        w_up,
        w_down.T,
    )


def solution(mesh, block=1024):
    return jax.shard_map(
        functools.partial(local, mesh.shape["ctx"], mesh.shape["head"], block),
        mesh=mesh,
        in_specs=(
            P("ctx", "head"),
            P("ctx", "head", None),
            P("ctx", "head", None),
            P("ctx"),
            P(),
            P(None, "ctx"),
            P("head", "ctx"),
            P("ctx"),
            P("ctx", "head"),
            P("ctx", "head"),
            P("head", "ctx"),
        ),
        out_specs=(P("ctx", "head"), P(None, "ctx"), P("head", "ctx")),
        check_vma=False,
    )
```

time: 570 us -> 92 us (0.16)
  blocking collectives: 192 us -> 0 us
  waiting for transfers between devices: 154 us -> 0 us
  matrix products: 98 us -> 0 us
  Pallas kernels: 0 us -> 85.2 us
  other arithmetic: 52.9 us -> 0 us
  local copies, waits for them, and re-layouts: 32.3 us -> 5.25 us
  loops' own time: 21.6 us -> 0 us
  between operations: 14.6 us -> 1.29 us
    psum x3 -> x0, waiting for transfers between devices: 154 us -> none  [the longest x1 57.6 us: local(): mixed = lax.psum(projected, 'head')]
    dot_general x36 -> x0, matrix products: 98 us -> none  [the longest x16 59.1 us: visit(): jnp.einsum('hrd,khd->hrk', query_heads, key_block, preferred_element_type...]
    psum x2 -> x0, blocking collectives: 89.3 us -> none  [the longest x1 55.8 us: local(): lax.psum((row_acc * rescale[:, :, None], row_total * rescale), 'ctx')]
    pallas_call x0 -> x1, Pallas kernels: none -> 85.2 us  [local(): pl.pallas_call(functools.partial(kernel, sizes), out_shape=(jax.ShapeDtyp...]
    pmax x1 -> x0, blocking collectives: 57.9 us -> none  [local(): top_score = lax.pmax(row_high, 'ctx')]
    reduce_sum x17 -> x0, other arithmetic: 49.2 us -> none  [the longest x16 47.5 us: visit(): row_total = row_total * rescale + jnp.sum(weights, axis=2)]
    unnamed x1 -> x0, blocking collectives: 23.6 us -> none
    another operation x1 -> x0, loops' own time: 21.6 us -> none  [local(): lax.scan(visit, (start_high, start_total, start_acc), jnp.arange(turns, d...]
  transfers between devices with their start and end apart: 3 -> 0, of which waited for: 3 -> 0; matrix products, arithmetic and copies ran while one was open for 0% -> 0% of each run, Pallas kernels for 0% -> 0%
where the time goes in v1:
time: 92 us; the launch traced here: 91.7 us
  Pallas kernels  85.2 us (93%)
  local copies, waits for them, and re-layouts  5.25 us (6%)
  between operations  1.29 us (1%)
    pallas_call x1, Pallas kernels, local(): pl.pallas_call(functools.partial(kernel, sizes), out_shape=(jax.ShapeDtyp...  85.2 us
    unnamed x3, local copies, waits for them, and re-layouts  4.01 us

profile of v1, /device:TPU:1, one launch (start us, length us, event | category | flops | bytes accessed | tf_op | source)
XLA Modules:
  0.0 91.7 jit_solution(17758065102173929484)
XLA Ops:
  1.3 1.2 %reshape.19.gain = f32[1,320]{1,0:T(1,128)} reshape(f32[320]{0:T(512)} %param.18) | data formatting | bytes 2560 | tf_op jit(solution)/shard_map/reshape | solution.py:513
  2.5 85.2 %layer.1 = (bf16[4,1024]{1,0:T(4,128)(2,1)}, bf16[64,320]{1,0:T(8,128)(2,1)}, bf16[8,320]{1,0:T(8,128)(2,1)}) custom-call(bf16[4,1024]{1,0:T(4,128)(2,1)} %queries.1, s32[1,64]{1,0:T(1,128)} %bitcast.9, s32[1]{0:T(128)S(6)} %copy.17.offsets, bf16[64,320]{1,0:T(8,128)(2,1)} %residual.1, f32[1,320]{1,0:T(1,128)} %reshape.19.gain, bf16[32768,128]{1,0:T(8,128)(2,1)} %bitcast.5, ...), custom_call_target="tpu_custom_call" | custom-call | tf_op jit(solution)/shard_map/layer/pallas_call | solution.py:458
  87.7 1.3 %copy.18 = bf16[4,1024]{1,0:T(4,128)(2,1)} copy(bf16[4,1024]{1,0:T(4,128)(2,1)} %get-tuple-element.6) | data formatting | bytes 16384
  89.0 1.4 %copy.19 = bf16[64,320]{1,0:T(8,128)(2,1)} copy(bf16[64,320]{1,0:T(8,128)(2,1)} %get-tuple-element.7) | data formatting | bytes 81920
  90.4 1.3 %copy.20 = bf16[8,320]{1,0:T(8,128)(2,1)} copy(bf16[8,320]{1,0:T(8,128)(2,1)} %get-tuple-element.8) | data formatting | bytes 10240

commit v2 on v1

--- a/solution.py
+++ b/solution.py
@@ -16,6 +16,9 @@
 GROUPS = 8
 HEAD = 128
 LANES = 128
+EARLY = 16
+GRANT = 60 * 1024 * 1024
+PIECES = 2
 
 
 def dot(a, b):
@@ -26,13 +29,18 @@
     return lax.dot_general(a, b, (((1,), (1,)), ((), ())), preferred_element_type=F32)
 
 
+def cuts_of(first):
+    step = first // LANES // PIECES // 2 * 2 * LANES
+    return [k * step for k in range(PIECES)] + [first]
+
+
 def kernel(
     sizes,
-    queries,
-    lengths,
     offsets,
-    residual,
-    gain,
+    queries_in,
+    lengths_in,
+    residual_in,
+    gain_in,
     keys,
     values,
     wo,
@@ -42,6 +50,10 @@
     attended,
     stream,
     ffn_out,
+    queries,
+    lengths,
+    residual,
+    gain,
     key_buf,
     value_buf,
     wo_buf,
@@ -65,19 +77,19 @@
     proj_all,
     square_tile,
     lhs,
-    gate_send,
-    gate_recv,
-    hidden_send,
-    hidden_all,
     down_send,
     down_recv,
     load_sem,
     weight_sem,
+    small_sem,
     ctx_send,
     ctx_recv,
     head_send,
     head_recv,
+    *pieces,
 ):
+    pieces = [pieces[4 * i : 4 * i + 4] for i in range(len(pieces) // 4)]
+    cuts = cuts_of(pair_buf.shape[1])
     ctxs, heads, span, block, width, model = sizes
     batch = 4 * ctxs
     rows = batch * GROUPS
@@ -86,8 +98,23 @@
     first = pair_buf.shape[1]
     second = hidden_width - first
     base = 1.0 / math.sqrt(HEAD) * math.log2(math.e)
+    early = min(EARLY, turns)
     ctx = lax.axis_index("ctx")
     head = lax.axis_index("head")
+
+    far = lambda d, n: min(d, n - d)
+    sides = (4, 4) if ctxs == 16 else (1, ctxs)
+    steps = [(a, b) for a in range(sides[0]) for b in range(sides[1]) if a or b]
+    steps.sort(key=lambda t: -far(t[0], sides[0]) - far(t[1], sides[1]))
+    major, minor = ctx // sides[1], lax.rem(ctx, sides[1])
+    ctx_others = [
+        lax.rem(major + a, sides[0]) * sides[1] + lax.rem(minor + b, sides[1]) for a, b in steps
+    ]
+    chips = heads // 2
+    steps = [(a, b) for a in range(chips) for b in range(2) if a or b]
+    steps.sort(key=lambda t: -2 * far(t[0], chips) - t[1])
+    chip, core = head // 2, lax.rem(head, 2)
+    head_others = [lax.rem(chip + a, chips) * 2 + lax.rem(core + b, 2) for a, b in steps]
 
     def key_copy(c):
         part = pl.ds(pl.multiple_of(c * block, block), block)
@@ -118,92 +145,61 @@
         pltpu.make_async_copy(w_down, down_buf, weight_sem.at[5]),
     ]
 
+    small_copies = [
+        pltpu.make_async_copy(source, target, small_sem.at[i])
+        for i, (source, target) in enumerate(
+            (
+                (queries_in, queries),
+                (lengths_in, lengths),
+                (residual_in, residual),
+                (gain_in, gain),
+            )
+        )
+    ]
+
     barrier = pltpu.get_barrier_semaphore()
-
-    def greet_ctx(p, _):
-        pl.semaphore_signal(
-            barrier, inc=1, device_id={"ctx": lax.rem(ctx + p, ctxs)}, device_id_type=MESH
-        )
-        return 0
-
-    def greet_head(p, _):
-        pl.semaphore_signal(
-            barrier, inc=1, device_id={"head": lax.rem(head + p, heads)}, device_id_type=MESH
-        )
-        return 0
-
-    lax.fori_loop(1, ctxs, greet_ctx, 0)
-    lax.fori_loop(1, heads, greet_head, 0)
+    for other in ctx_others:
+        pl.semaphore_signal(barrier, inc=1, device_id={"ctx": other}, device_id_type=MESH)
+    for other in head_others:
+        pl.semaphore_signal(barrier, inc=1, device_id={"head": other}, device_id_type=MESH)
 
     def fetch(c, _):
         key_copy(c).start()
         value_copy(c).start()
         return 0
 
-    lax.fori_loop(0, turns, fetch, 0)
-    for copy in weight_copies:
-        copy.start()
-
-    def over_ctx(phase, source, slots):
+    small_copies[0].start()
+    lax.fori_loop(0, early, fetch, 0)
+
+    def exchange(axis, me, others, send_sems, recv_sems, phase, source, slots):
         def one(other, mine):
             return pltpu.make_async_remote_copy(
                 src_ref=source(other),
                 dst_ref=slots.at[mine],
-                send_sem=ctx_send.at[phase, other],
-                recv_sem=ctx_recv.at[phase, mine],
-                device_id={"ctx": other},
+                send_sem=send_sems.at[phase, other],
+                recv_sem=recv_sems.at[phase, mine],
+                device_id={axis: other},
                 device_id_type=MESH,
             )
 
-        def start(p, _):
-            one(lax.rem(ctx + p, ctxs), ctx).start()
-            return 0
-
-        def arrive(p, _):
-            other = lax.rem(ctx + ctxs - p, ctxs)
-            one(other, other).wait_recv()
-            return 0
-
-        def sent(p, _):
-            one(lax.rem(ctx + p, ctxs), ctx).wait_send()
-            return 0
-
-        return (
-            lambda: lax.fori_loop(1, ctxs, start, 0),
-            lambda: lax.fori_loop(1, ctxs, arrive, 0),
-            lambda: lax.fori_loop(1, ctxs, sent, 0),
-        )
-
-    def over_head(phase, source, slots):
-        def one(other, mine):
-            return pltpu.make_async_remote_copy(
-                src_ref=source(other),
-                dst_ref=slots.at[mine],
-                send_sem=head_send.at[phase, other],
-                recv_sem=head_recv.at[phase, mine],
-                device_id={"head": other},
-                device_id_type=MESH,
-            )
-
-        def start(p, _):
-            one(lax.rem(head + p, heads), head).start()
-            return 0
-
-        def arrive(p, _):
-            other = lax.rem(head + heads - p, heads)
-            one(other, other).wait_recv()
-            return 0
-
-        def sent(p, _):
-            one(lax.rem(head + p, heads), head).wait_send()
-            return 0
-
-        return (
-            lambda: lax.fori_loop(1, heads, start, 0),
-            lambda: lax.fori_loop(1, heads, arrive, 0),
-            lambda: lax.fori_loop(1, heads, sent, 0),
-        )
-
+        def start():
+            for other in others:
+                one(other, me).start()
+
+        def arrive():
+            for other in reversed(others):
+                one(other, other).wait_recv()
+
+        def sent():
+            for other in others:
+                one(other, me).wait_send()
+
+        return start, arrive, sent
+
+    over_ctx = functools.partial(exchange, "ctx", ctx, ctx_others, ctx_send, ctx_recv)
+    over_head = functools.partial(exchange, "head", head, head_others, head_send, head_recv)
+
+    small_copies[0].wait()
     own = queries[...].astype(F32)
     for g in range(GROUPS):
         query_row[pl.ds(g, 4, stride=GROUPS), :] = own[:, g * HEAD : (g + 1) * HEAD]
@@ -213,6 +209,13 @@
     pl.semaphore_wait(barrier, ctxs - 1 + heads - 1)
     q_start, q_arrive, q_sent = over_ctx(0, lambda other: query_send, query_all)
     q_start()
+    for copy in small_copies[1:]:
+        copy.start()
+    lax.fori_loop(early, turns, fetch, 0)
+    for copy in weight_copies:
+        copy.start()
+    for copy in small_copies[1:]:
+        copy.wait()
 
     visible[...] = jnp.full(visible.shape, 2**30, jnp.int32)
     visible[0:1, 0:batch] = lengths[...] - offsets[0]
@@ -347,7 +350,7 @@
     combined = combined + mixed
     stream[...] = combined.astype(BF16)
     squares = jnp.sum(combined * combined, axis=1, keepdims=True)
-    normed = (combined * gain[...]).astype(BF16)
+    normed = (combined * gain[...].reshape(1, width)).astype(BF16)
 
     tall = 16 * ctxs
     spread = jnp.where(
@@ -365,51 +368,67 @@
     s2 = squares - s1
     lane = lax.broadcasted_iota(jnp.int32, (batch, LANES), 1)
     marks = jnp.where(lane == 0, s1, jnp.where(lane == 1, s2, 0.0)).astype(BF16)
-    gate_send[:, :, first : first + LANES] = (
+    pieces[0][0][:, :, cuts[1] : cuts[1] + LANES] = (
         dot(spread, marks).astype(BF16).reshape(ctxs, 16, LANES)
     )
     for copy in weight_copies[1:5]:
         copy.wait()
     full = lhs[...]
-    for at in range(0, second, 256):
-        wide = min(256, second - at)
-        gate_send[:, :, at : at + wide] = (
-            dot(full, pair_buf[:, at : at + wide]).astype(BF16).reshape(ctxs, 16, wide)
-        )
-    gate_send[:, :, second:first] = (
-        dot(full[:, 0 : 2 * width], pair_buf[0 : 2 * width, second:first])
-        .astype(BF16)
-        .reshape(ctxs, 16, first - second)
-    )
-    gate_recv[ctx] = gate_send[ctx]
-    g_start, g_arrive, g_sent = over_ctx(3, lambda other: gate_send.at[other], gate_recv)
-    g_start()
+
+    gates = []
+    hiddens = []
+    for k, (gate_send, gate_recv, hidden_send, hidden_all) in enumerate(pieces):
+        low, top = cuts[k : k + 2]
+        for at in range(low, min(top, second), 256):
+            wide = min(256, min(top, second) - at)
+            gate_send[:, :, at - low : at - low + wide] = (
+                dot(full, pair_buf[:, at : at + wide]).astype(BF16).reshape(ctxs, 16, wide)
+            )
+        if top > second:
+            gate_send[:, :, second - low : top - low] = (
+                dot(full[:, 0 : 2 * width], pair_buf[0 : 2 * width, second:top])
+                .astype(BF16)
+                .reshape(ctxs, 16, top - second)
+            )
+        gate_recv[ctx] = gate_send[ctx]
+        gates.append(over_ctx(3 + k, lambda other, sent=gate_send: sent.at[other], gate_recv))
+        gates[k][0]()
     d_sent()
-    g_arrive()
-
-    summed = gate_recv[0].astype(F32)
-    for i in range(1, ctxs):
-        summed = summed + gate_recv[i].astype(F32)
-    square_total = jnp.sum(summed[:, first : first + LANES], axis=1, keepdims=True)
-    scaled = summed[:, 0:first] * lax.rsqrt(square_total / model + EPSILON)
 
     def gated(v):
         return v / (1.0 + jnp.exp(-v)) * pltpu.roll(v, 4, 0)
 
-    upper = gated(scaled[0:8])
-    lower = gated(scaled[8:16])
-    index = lax.broadcasted_iota(jnp.int32, (8, first), 0)
-    hidden_send[...] = jnp.where(index < 4, upper, pltpu.roll(lower, 4, 0)).astype(BF16)
-    hidden_all[ctx] = hidden_send[...]
-    h_start, h_arrive, h_sent = over_ctx(4, lambda other: hidden_send, hidden_all)
-    h_start()
-    g_sent()
+    for k, (gate_send, gate_recv, hidden_send, hidden_all) in enumerate(pieces):
+        low, top = cuts[k : k + 2]
+        gates[k][1]()
+        summed = gate_recv[0].astype(F32)
+        for i in range(1, ctxs):
+            summed = summed + gate_recv[i].astype(F32)
+        if k == 0:
+            square_total = jnp.sum(
+                summed[:, top : top + LANES], axis=1, keepdims=True
+            )
+            scale = lax.rsqrt(square_total / model + EPSILON)
+        scaled = summed[:, 0 : top - low] * scale
+        upper = gated(scaled[0:8])
+        lower = gated(scaled[8:16])
+        index = lax.broadcasted_iota(jnp.int32, upper.shape, 0)
+        hidden_send[...] = jnp.where(index < 4, upper, pltpu.roll(lower, 4, 0)).astype(BF16)
+        hidden_all[ctx] = hidden_send[...]
+        hiddens.append(
+            over_ctx(3 + len(pieces) + k, lambda other, sent=hidden_send: sent, hidden_all)
+        )
+        hiddens[k][0]()
     weight_copies[5].wait()
-    h_arrive()
-
-    hidden = hidden_all[...].astype(F32).reshape(8 * ctxs, first).astype(BF16)
-    one = dot_across(hidden, down_buf[:, 0:first])
-    two = dot_across(hidden[:, 0:second], down_buf[:, first:hidden_width])
+    one = jnp.zeros((8 * ctxs, width), F32)
+    two = jnp.zeros((8 * ctxs, width), F32)
+    for k, (gate_send, gate_recv, hidden_send, hidden_all) in enumerate(pieces):
+        low, top = cuts[k : k + 2]
+        hiddens[k][1]()
+        hidden = hidden_all[...].astype(F32).reshape(8 * ctxs, top - low).astype(BF16)
+        one = one + dot_across(hidden, down_buf[:, low:top])
+        rest = min(top, second) - low
+        two = two + dot_across(hidden[:, 0:rest], down_buf[:, first + low : first + low + rest])
     both = one + pltpu.roll(two, 8 * ctxs - 4, 0)
     index = lax.broadcasted_iota(jnp.int32, (8, width), 0)
     for i in range(heads):
@@ -417,17 +436,30 @@
             index < 4,
             both[16 * i : 16 * i + 8],
             pltpu.roll(both[16 * i + 8 : 16 * i + 16], 4, 0),
-        )
+        ).astype(BF16)
     down_recv[head] = down_send[head]
     f_start, f_arrive, f_sent = over_head(1, lambda other: down_send.at[other], down_recv)
     f_start()
-    h_sent()
+    for k in range(len(pieces)):
+        gates[k][2]()
+        hiddens[k][2]()
     f_arrive()
-    result = down_recv[0]
+    result = down_recv[0].astype(F32)
     for i in range(1, heads):
-        result = result + down_recv[i]
+        result = result + down_recv[i].astype(F32)
     ffn_out[...] = result.astype(BF16)
     f_sent()
+
+
+def hand_over(a_in, b_in, c_in, a, b, c, sem):
+    copies = [
+        pltpu.make_async_copy(source, target, sem.at[i])
+        for i, (source, target) in enumerate(((a_in, a), (b_in, b), (c_in, c)))
+    ]
+    for copy in copies:
+        copy.start()
+    for copy in copies:
+        copy.wait()
 
 
 def local(
@@ -451,20 +483,37 @@
     rows = batch * GROUPS
     hidden_width = w_gate.shape[1]
     first = (hidden_width // LANES + 1) // 2 * LANES
+    cuts = cuts_of(first)
+    slabs = []
+    for k in range(PIECES):
+        wide = cuts[k + 1] - cuts[k]
+        more = 0 if k else LANES
+        slabs += [
+            pltpu.VMEM((ctxs, 16, wide + more), BF16),
+            pltpu.VMEM((ctxs, 16, wide + more), BF16),
+            pltpu.VMEM((8, wide), BF16),
+            pltpu.VMEM((ctxs, 8, wide), BF16),
+        ]
     sizes = (ctxs, heads, span, block, width, width * ctxs)
     vmem = pl.BlockSpec(memory_space=pltpu.VMEM)
+    hbm = pl.BlockSpec(memory_space=pltpu.HBM)
     smem = pl.BlockSpec(memory_space=pltpu.SMEM)
-    hbm = pl.BlockSpec(memory_space=pl.ANY)
-    return pl.pallas_call(
+    free = pl.BlockSpec(memory_space=pl.ANY)
+    outs = (
+        jax.ShapeDtypeStruct(queries.shape, BF16),
+        jax.ShapeDtypeStruct((batch, width), BF16),
+        jax.ShapeDtypeStruct((batch // heads, width), BF16),
+    )
+    results = pl.pallas_call(
         functools.partial(kernel, sizes),
-        out_shape=(
-            jax.ShapeDtypeStruct(queries.shape, BF16),
-            jax.ShapeDtypeStruct((batch, width), BF16),
-            jax.ShapeDtypeStruct((batch // heads, width), BF16),
-        ),
-        in_specs=[vmem, vmem, smem, vmem, vmem] + [hbm] * 6,
+        out_shape=tuple(pltpu.VMEM(o.shape, o.dtype) for o in outs),
+        in_specs=[smem] + [hbm] * 10,
         out_specs=(vmem, vmem, vmem),
         scratch_shapes=[
+            pltpu.VMEM(queries.shape, BF16),
+            pltpu.VMEM((1, batch), jnp.int32),
+            pltpu.VMEM(residual.shape, BF16),
+            pltpu.VMEM((width,), F32),
             pltpu.VMEM((span, HEAD), BF16),
             pltpu.VMEM((span, HEAD), BF16),
             pltpu.VMEM((width, rows * HEAD // batch), BF16),
@@ -488,39 +537,51 @@
             pltpu.VMEM((heads, batch, width), BF16),
             pltpu.VMEM((LANES, LANES), F32),
             pltpu.VMEM((16 * ctxs, 4 * width), BF16),
-            pltpu.VMEM((ctxs, 16, first + LANES), BF16),
-            pltpu.VMEM((ctxs, 16, first + LANES), BF16),
-            pltpu.VMEM((8, first), BF16),
-            pltpu.VMEM((ctxs, 8, first), BF16),
-            pltpu.VMEM((heads, 8, width), F32),
-            pltpu.VMEM((heads, 8, width), F32),
+            pltpu.VMEM((heads, 8, width), BF16),
+            pltpu.VMEM((heads, 8, width), BF16),
             pltpu.SemaphoreType.DMA((2, span // block)),
             pltpu.SemaphoreType.DMA((6,)),
-            pltpu.SemaphoreType.DMA((5, ctxs)),
-            pltpu.SemaphoreType.DMA((5, ctxs)),
+            pltpu.SemaphoreType.DMA((4,)),
+            pltpu.SemaphoreType.DMA((3 + 2 * PIECES, ctxs)),
+            pltpu.SemaphoreType.DMA((3 + 2 * PIECES, ctxs)),
             pltpu.SemaphoreType.DMA((2, heads)),
             pltpu.SemaphoreType.DMA((2, heads)),
-        ],
+        ]
+        + slabs,
         compiler_params=pltpu.CompilerParams(
-            collective_id=0, has_side_effects=True, vmem_limit_bytes=60 * 1024 * 1024
+            collective_id=0, has_side_effects=True, vmem_limit_bytes=GRANT
         ),
         name="layer",
     )(
-        queries,
-        lengths.reshape(1, batch),
         offsets,
-        residual,
-        norm_gain.reshape(1, width),
-        keys.reshape(span, HEAD),
-        values.reshape(span, HEAD),
-        wo.T,
-        w_gate,
-        w_up,
-        w_down.T,
+        *(
+            pltpu.with_memory_space_constraint(x, pltpu.HBM)
+            for x in (
+                queries,
+                lengths.reshape(1, batch),
+                residual,
+                norm_gain,
+                keys.reshape(span, HEAD),
+                values.reshape(span, HEAD),
+                wo.T,
+                w_gate,
+                w_up,
+                w_down.T,
+            )
+        )
     )
-
-
-def solution(mesh, block=1024):
+    return pl.pallas_call(
+        hand_over,
+        out_shape=outs,
+        in_specs=[free] * 3,
+        out_specs=(free,) * 3,
+        scratch_shapes=[pltpu.SemaphoreType.DMA((3,))],
+        compiler_params=pltpu.CompilerParams(vmem_limit_bytes=1024 * 1024),
+        name="hand_over",
+    )(*results)
+
+
+def solution(mesh, block=2048):
     return jax.shard_map(
         functools.partial(local, mesh.shape["ctx"], mesh.shape["head"], block),
         mesh=mesh,

time: 92 us -> 78.2 us (0.85)
  Pallas kernels: 85.2 us -> 76.8 us
  local copies, waits for them, and re-layouts: 5.25 us -> 0 us
    pallas_call x1 -> x2, Pallas kernels: 85.2 us -> 76.8 us  [the longest x1 76.1 us: local(): pl.pallas_call(functools.partial(kernel, sizes), out_shape=tuple((pltpu.V...]
    unnamed x3 -> x0, local copies, waits for them, and re-layouts: 4.01 us -> none
    reshape x1 -> x0, local copies, waits for them, and re-layouts: 1.25 us -> none  [local(): norm_gain.reshape(1, width)]
where the time goes in v2:
time: 78.2 us; the launch traced here: 78.1 us
  Pallas kernels  76.8 us (98%)
  between operations  1.29 us (2%)
    pallas_call x1, Pallas kernels, local(): pl.pallas_call(functools.partial(kernel, sizes), out_shape=tuple((pltpu.V...  76.1 us

profile of v2, /device:TPU:1, one launch (start us, length us, event | category | flops | bytes accessed | tf_op | source)
XLA Modules:
  0.0 78.1 jit_solution(7632937010557967657)
XLA Ops:
  1.3 76.1 %layer.1 = (bf16[4,1024]{1,0:T(4,128)(2,1)S(1)}, bf16[64,320]{1,0:T(8,128)(2,1)S(1)}, bf16[8,320]{1,0:T(8,128)(2,1)S(1)}) custom-call(s32[1]{0:T(128)S(6)} %copy.14.offsets, bf16[4,1024]{1,0:T(4,128)(2,1)} %queries_in.1, s32[1,64]{1,0:T(1,128)} %bitcast.9, bf16[64,320]{1,0:T(8,128)(2,1)} %residual_in.1, f32[320]{0:T(512)} %gain_in.1, ...), custom_call_target="tpu_custom_call" | custom-call | tf_op jit(solution)/shard_map/layer/pallas_call | solution.py:507
  77.4 0.7 hand_over.1

commit v3 on v2

--- a/solution.py
+++ b/solution.py
@@ -31,7 +31,8 @@
 
 def cuts_of(first):
     step = first // LANES // PIECES // 2 * 2 * LANES
-    return [k * step for k in range(PIECES)] + [first]
+    edges = [k * step for k in range(PIECES)] + [first]
+    return [(edges[k], edges[k + 1]) for k in reversed(range(PIECES))]
 
 
 def kernel(
@@ -277,7 +278,7 @@
     high_row = high[0:1, :]
     total_row = total[0:1, :]
     part_send[:, 0:32, :] = (
-        (acc[...] / total_row).T.astype(BF16).reshape(ctxs, 32, HEAD)
+        (acc[...] / total_row).astype(BF16).T.reshape(ctxs, 32, HEAD)
     )
 
     def piece(v):
@@ -332,22 +333,32 @@
     weight_copies[0].wait()
     r_arrive()
 
+    kept = width - 64
+    quarter = batch // 4
+
+    def pack(v):
+        parts = [v[i * quarter : (i + 1) * quarter, kept:width] for i in range(4)]
+        return jnp.concatenate([v[:, 0:kept], jnp.concatenate(parts, axis=1)], axis=0)
+
+    def unpack(v):
+        parts = [v[batch : batch + quarter, i * 64 : (i + 1) * 64] for i in range(4)]
+        return jnp.concatenate([v[0:batch], jnp.concatenate(parts, axis=0)], axis=1)
+
     wide_f32[...] = rows_all[...].astype(F32).reshape(rows, HEAD)
     projected = jnp.zeros((batch, width), F32)
     for g in range(GROUPS):
         lines = wide_f32[pl.ds(g, batch, stride=GROUPS), :].astype(BF16)
         projected = projected + dot_across(lines, wo_buf[:, g * HEAD : (g + 1) * HEAD])
-    proj_all[head] = projected.astype(BF16)
+    proj_all[head] = pack(projected).astype(BF16)
     d_start, d_arrive, d_sent = over_head(0, lambda other: proj_all.at[head], proj_all)
     d_start()
     r_sent()
     d_arrive()
 
-    combined = residual[...].astype(F32)
     mixed = proj_all[0].astype(F32)
     for i in range(1, heads):
         mixed = mixed + proj_all[i].astype(F32)
-    combined = combined + mixed
+    combined = residual[...].astype(F32) + unpack(mixed)
     stream[...] = combined.astype(BF16)
     squares = jnp.sum(combined * combined, axis=1, keepdims=True)
     normed = (combined * gain[...].reshape(1, width)).astype(BF16)
@@ -368,9 +379,7 @@
     s2 = squares - s1
     lane = lax.broadcasted_iota(jnp.int32, (batch, LANES), 1)
     marks = jnp.where(lane == 0, s1, jnp.where(lane == 1, s2, 0.0)).astype(BF16)
-    pieces[0][0][:, :, cuts[1] : cuts[1] + LANES] = (
-        dot(spread, marks).astype(BF16).reshape(ctxs, 16, LANES)
-    )
+    marks = dot(spread, marks)
     for copy in weight_copies[1:5]:
         copy.wait()
     full = lhs[...]
@@ -378,7 +387,7 @@
     gates = []
     hiddens = []
     for k, (gate_send, gate_recv, hidden_send, hidden_all) in enumerate(pieces):
-        low, top = cuts[k : k + 2]
+        low, top = cuts[k]
         for at in range(low, min(top, second), 256):
             wide = min(256, min(top, second) - at)
             gate_send[:, :, at - low : at - low + wide] = (
@@ -386,7 +395,11 @@
             )
         if top > second:
             gate_send[:, :, second - low : top - low] = (
-                dot(full[:, 0 : 2 * width], pair_buf[0 : 2 * width, second:top])
+                jnp.where(
+                    lax.broadcasted_iota(jnp.int32, (tall, LANES), 0) % 16 < 8,
+                    dot(full[:, 0 : 2 * width], pair_buf[0 : 2 * width, second:top]),
+                    marks,
+                )
                 .astype(BF16)
                 .reshape(ctxs, 16, top - second)
             )
@@ -399,16 +412,15 @@
         return v / (1.0 + jnp.exp(-v)) * pltpu.roll(v, 4, 0)
 
     for k, (gate_send, gate_recv, hidden_send, hidden_all) in enumerate(pieces):
-        low, top = cuts[k : k + 2]
+        low, top = cuts[k]
         gates[k][1]()
         summed = gate_recv[0].astype(F32)
         for i in range(1, ctxs):
             summed = summed + gate_recv[i].astype(F32)
         if k == 0:
-            square_total = jnp.sum(
-                summed[:, top : top + LANES], axis=1, keepdims=True
-            )
+            square_total = jnp.sum(summed[8:16, second - low : top - low], axis=1, keepdims=True)
             scale = lax.rsqrt(square_total / model + EPSILON)
+            scale = jnp.concatenate([scale, scale], axis=0)
         scaled = summed[:, 0 : top - low] * scale
         upper = gated(scaled[0:8])
         lower = gated(scaled[8:16])
@@ -423,7 +435,7 @@
     one = jnp.zeros((8 * ctxs, width), F32)
     two = jnp.zeros((8 * ctxs, width), F32)
     for k, (gate_send, gate_recv, hidden_send, hidden_all) in enumerate(pieces):
-        low, top = cuts[k : k + 2]
+        low, top = cuts[k]
         hiddens[k][1]()
         hidden = hidden_all[...].astype(F32).reshape(8 * ctxs, top - low).astype(BF16)
         one = one + dot_across(hidden, down_buf[:, low:top])
@@ -486,11 +498,10 @@
     cuts = cuts_of(first)
     slabs = []
     for k in range(PIECES):
-        wide = cuts[k + 1] - cuts[k]
-        more = 0 if k else LANES
+        wide = cuts[k][1] - cuts[k][0]
         slabs += [
-            pltpu.VMEM((ctxs, 16, wide + more), BF16),
-            pltpu.VMEM((ctxs, 16, wide + more), BF16),
+            pltpu.VMEM((ctxs, 16, wide), BF16),
+            pltpu.VMEM((ctxs, 16, wide), BF16),
             pltpu.VMEM((8, wide), BF16),
             pltpu.VMEM((ctxs, 8, wide), BF16),
         ]
@@ -534,7 +545,7 @@
             pltpu.VMEM((32, HEAD), BF16),
             pltpu.VMEM((ctxs, 32, HEAD), BF16),
             pltpu.VMEM((rows, HEAD), F32),
-            pltpu.VMEM((heads, batch, width), BF16),
+            pltpu.VMEM((heads, batch + batch // 4, 256), BF16),
             pltpu.VMEM((LANES, LANES), F32),
             pltpu.VMEM((16 * ctxs, 4 * width), BF16),
             pltpu.VMEM((heads, 8, width), BF16),
@@ -581,7 +592,7 @@
     )(*results)
 
 
-def solution(mesh, block=2048):
+def solution(mesh, block=4096):
     return jax.shard_map(
         functools.partial(local, mesh.shape["ctx"], mesh.shape["head"], block),
         mesh=mesh,

time: 78.2 us -> 75.7 us (0.968)
  Pallas kernels: 76.8 us -> 74.1 us
    pallas_call x1, Pallas kernels: 76.1 us -> 73.5 us  [local(): pl.pallas_call(functools.partial(kernel, sizes), out_shape=tuple((pltpu.V...]
where the time goes in v3:
time: 75.7 us; the launch traced here: 75.6 us
  Pallas kernels  74.1 us (98%)
  between operations  1.45 us (2%)
    pallas_call x1, Pallas kernels, local(): pl.pallas_call(functools.partial(kernel, sizes), out_shape=tuple((pltpu.V...  73.5 us

profile of v3, /device:TPU:1, one launch (start us, length us, event | category | flops | bytes accessed | tf_op | source)
XLA Modules:
  0.0 75.6 jit_solution(3192796269211238104)
XLA Ops:
  1.3 73.5 %layer.1 = (bf16[4,1024]{1,0:T(4,128)(2,1)S(1)}, bf16[64,320]{1,0:T(8,128)(2,1)S(1)}, bf16[8,320]{1,0:T(8,128)(2,1)S(1)}) custom-call(s32[1]{0:T(128)S(6)} %copy.14.offsets, bf16[4,1024]{1,0:T(4,128)(2,1)} %queries_in.1, s32[1,64]{1,0:T(1,128)} %bitcast.9, bf16[64,320]{1,0:T(8,128)(2,1)} %residual_in.1, f32[320]{0:T(512)} %gain_in.1, ...), custom_call_target="tpu_custom_call" | custom-call | tf_op jit(solution)/shard_map/layer/pallas_call | solution.py:518
  74.8 0.7 hand_over.1

commit v4 on v3

--- a/solution.py
+++ b/solution.py
@@ -78,6 +78,7 @@
     proj_all,
     square_tile,
     lhs,
+    spread_buf,
     down_send,
     down_recv,
     load_sem,
@@ -226,6 +227,14 @@
     row_of = lax.broadcasted_iota(jnp.int32, (rows, LANES), 0) // GROUPS
     column = lax.broadcasted_iota(jnp.int32, (rows, LANES), 1)
     query_wide[:, HEAD : HEAD + LANES] = jnp.where(row_of == column, HIDDEN_SCORE, 0.0).astype(BF16)
+    tall = 16 * ctxs
+    spread_buf[...] = jnp.where(
+        lax.broadcasted_iota(jnp.int32, (tall, batch), 0) // 16 * 4
+        + lax.broadcasted_iota(jnp.int32, (tall, batch), 0) % 4
+        == lax.broadcasted_iota(jnp.int32, (tall, batch), 1),
+        1.0,
+        0.0,
+    ).astype(BF16)
     q_arrive()
     query_wide[:, 0:HEAD] = query_all[...].reshape(rows, HEAD)
 
@@ -363,14 +372,7 @@
     squares = jnp.sum(combined * combined, axis=1, keepdims=True)
     normed = (combined * gain[...].reshape(1, width)).astype(BF16)
 
-    tall = 16 * ctxs
-    spread = jnp.where(
-        lax.broadcasted_iota(jnp.int32, (tall, batch), 0) // 16 * 4
-        + lax.broadcasted_iota(jnp.int32, (tall, batch), 0) % 4
-        == lax.broadcasted_iota(jnp.int32, (tall, batch), 1),
-        1.0,
-        0.0,
-    ).astype(BF16)
+    spread = spread_buf[...]
     copies = dot(spread, normed)
     which = lax.broadcasted_iota(jnp.int32, (tall, width), 0) % 16 // 4
     for k in range(4):
@@ -548,6 +550,7 @@
             pltpu.VMEM((heads, batch + batch // 4, 256), BF16),
             pltpu.VMEM((LANES, LANES), F32),
             pltpu.VMEM((16 * ctxs, 4 * width), BF16),
+            pltpu.VMEM((16 * ctxs, batch), BF16),
             pltpu.VMEM((heads, 8, width), BF16),
             pltpu.VMEM((heads, 8, width), BF16),
             pltpu.SemaphoreType.DMA((2, span // block)),

time: 75.7 us -> 75.7 us (level)
  no operation moved by 1% of the time
where the time goes in v4:
time: 75.7 us; the launch traced here: 75.5 us
  Pallas kernels  74.1 us (98%)
  between operations  1.45 us (2%)
    pallas_call x1, Pallas kernels, local(): pl.pallas_call(functools.partial(kernel, sizes), out_shape=tuple((pltpu.V...  73.4 us

profile of v4, /device:TPU:1, one launch (start us, length us, event | category | flops | bytes accessed | tf_op | source)
XLA Modules:
  0.0 75.5 jit_solution(3967352366460490381)
XLA Ops:
  1.3 73.4 %layer.1 = (bf16[4,1024]{1,0:T(4,128)(2,1)S(1)}, bf16[64,320]{1,0:T(8,128)(2,1)S(1)}, bf16[8,320]{1,0:T(8,128)(2,1)S(1)}) custom-call(s32[1]{0:T(128)S(6)} %copy.14.offsets, bf16[4,1024]{1,0:T(4,128)(2,1)} %queries_in.1, s32[1,64]{1,0:T(1,128)} %bitcast.9, bf16[64,320]{1,0:T(8,128)(2,1)} %residual_in.1, f32[320]{0:T(512)} %gain_in.1, ...), custom_call_target="tpu_custom_call" | custom-call | tf_op jit(solution)/shard_map/layer/pallas_call | solution.py:520
  74.7 0.7 hand_over.1
